TPU v7x, 512 devices: a whole 4x4x16 slice. The times are simulated.
512 devices in a mesh: sector: 16 (over y, x), grp: 32 (over z, core).
Axes of the slice: x: 4, y: 4, z: 16, core: 2. Of those that a mesh axis runs over, the one named last changes fastest.
Arguments:
- start_vector: bfloat16 [8192, 512], P(('sector', 'grp')), may hold values from -130 to 130
- tile_live: int32 [64], P('sector'), may hold values from 32 to 128, as said below
- env_blocks: bfloat16 [64, 384, 128, 128], P('grp', 'sector'), may hold values from -2 to 4
- block_owner: int32 [64, 384, 1], P('grp', 'sector'), may hold values from 0 to 15; in each aligned block of 24 rows (0 to 23, 24 to 47, ..., all dimensions but the last counted through in order) at most 2 rows name the same one
- block_rows: int32 [64, 384], P('grp', 'sector'), may hold values from 0 to 3
- block_cols: int32 [64, 384], P('grp', 'sector'), may hold values from 0 to 3
- site_left: bfloat16 [64, 1024], P('grp'), may hold values from -0.375 to 0.375
- mpo_pattern: int32 [64, 64], P('grp'), may hold values 0 or 1
- site_right: bfloat16 [64, 1024], P('grp'), may hold values from -0.375 to 0.375
- right_env: bfloat16 [64, 1024], P('grp'), may hold values from -0.125 to 0.125
Outputs:
- first_product: bfloat16 [8192, 512], P(('sector', 'grp'))
- second_product: bfloat16 [8192, 512], P(('sector', 'grp'))
Inputs may be any that keep to these rules, and one draw needn't show every extreme that they name: `tile_live`: rows beyond a tile's live count are padding; some tile is full. `block_owner`: in each aligned block of 24 entries of one channel (the blocks one device holds), no owner is named more than 2 times.
All inputs are finite; a program needn't handle non-finite values. No bound on the sum of `mpo_pattern` on one device may be relied on, other than what follows from the above.
Results may differ from a plain program's by a relative error of at most 0.03.
Values may be sent and summed in bfloat16 or wider, within the bound.
A program may use at most 64 MiB of HBM per device.

v0:
```python
import jax
import jax.numpy as jnp
from jax import lax
from jax.sharding import PartitionSpec as P

WM = 64
D1 = 4
RB = 32
TR = 128
TPO = 4
CAP = 2
PHYS = 16
epsilon = 1e-06


def contract(owned_rows, got_blocks, got_codes):
    channels = got_blocks.shape[0]
    slot_count = got_blocks.shape[1] * got_blocks.shape[2]
    results = []
    for channel in range(channels):
        blocks = got_blocks[channel].reshape(slot_count, TR * TR)
        slot_codes = got_codes[channel].reshape(slot_count)
        tile_index = jnp.maximum(slot_codes - 1, 0)
        pair_hot = (
            (tile_index[:, None] == jnp.arange(TPO * TPO, dtype=jnp.int32)[None, :])
            & (slot_codes[:, None] > 0)
        ).astype(jnp.bfloat16)
        summed = jnp.einsum(
            "sp,sq->pq", pair_hot, blocks, preferred_element_type=jnp.float32
        ).astype(jnp.bfloat16)
        dense = summed.reshape(TPO, TPO, TR, TR).transpose(0, 2, 1, 3).reshape(TPO * TR, TPO * TR)
        product = jnp.dot(dense, owned_rows, preferred_element_type=jnp.float32)
        results.append(product.astype(jnp.bfloat16))
    return jnp.stack(results)


def owner_gather(share_rows):
    return lax.all_gather(share_rows, "grp", axis=0, tiled=True)


def channel_share(mixed_rows, mixing):
    return lax.psum_scatter(
        jnp.einsum("wrk,wkn->rn", mixed_rows, mixing, preferred_element_type=jnp.float32).astype(
            jnp.bfloat16
        ),
        "grp",
        scatter_dimension=0,
        tiled=True,
    ).astype(jnp.float32)


def local(
    start_vector,
    tile_live,
    env_blocks,
    block_owner,
    block_rows,
    block_cols,
    site_left,
    mpo_pattern,
    site_right,
    right_env,
):
    sectors = lax.axis_size("sector")
    groups = lax.axis_size("grp")
    share_count = start_vector.shape[0]
    columns = start_vector.shape[1]
    channels = env_blocks.shape[0]
    held_blocks = env_blocks.shape[1]
    right_site, right_panels = (
        lax.all_gather(site_right, "grp", axis=0, tiled=True),
        lax.all_gather(right_env, "grp", axis=0, tiled=True),
    )
    left_site = (
        site_left.reshape(channels, WM, D1, D1) * mpo_pattern.astype(jnp.bfloat16)[:, :, None, None]
    )
    joined = jnp.einsum(
        "wmac,mxbd->wxabcd",
        left_site,
        right_site.reshape(WM, WM, D1, D1),
        preferred_element_type=jnp.float32,
    ).astype(jnp.bfloat16)
    mixing = jnp.einsum(
        "wxq,xr->wqr",
        joined.reshape(channels, WM, PHYS * PHYS),
        right_panels,
        preferred_element_type=jnp.float32,
    ).astype(jnp.bfloat16)
    mixing = (
        mixing.reshape(channels, PHYS, PHYS, RB, RB)
        .transpose(0, 2, 3, 1, 4)
        .reshape(channels, columns, columns)
    )
    owners = block_owner[:, :, 0]
    owner_hot = (owners[:, :, None] == jnp.arange(sectors, dtype=jnp.int32)[None, None, :]).astype(
        jnp.int32
    )
    position = jnp.sum((jnp.cumsum(owner_hot, axis=1) - owner_hot) * owner_hot, axis=2)
    slot_index = owners * CAP + position
    select = slot_index[:, :, None] == jnp.arange(sectors * CAP, dtype=jnp.int32)[None, None, :]
    packed = jnp.einsum(
        "wes,wen->wsn",
        select.astype(jnp.bfloat16),
        env_blocks.reshape(channels, held_blocks, TR * TR),
        preferred_element_type=jnp.float32,
    ).astype(jnp.bfloat16)
    slot_codes = jnp.sum(
        select.astype(jnp.int32) * (1 + block_rows * TPO + block_cols)[:, :, None], axis=1
    )
    got_blocks, got_codes = (
        lax.all_to_all(
            packed.reshape(channels, sectors, CAP, TR * TR),
            "sector",
            split_axis=1,
            concat_axis=1,
            tiled=True,
        ),
        lax.all_to_all(
            slot_codes.reshape(channels, sectors, CAP),
            "sector",
            split_axis=1,
            concat_axis=1,
            tiled=True,
        ),
    )
    tile_mask = (jnp.arange(TR, dtype=jnp.int32)[None, :] < tile_live[:, None]).reshape(TPO * TR)
    owner_mask = tile_mask.astype(jnp.float32)[:, None]
    share_mask = lax.dynamic_slice_in_dim(
        owner_mask, lax.axis_index("grp") * share_count, share_count, 0
    )
    entry_count = float(sectors * groups * share_count * columns)
    owned_rows = owner_gather(start_vector) * owner_mask.astype(jnp.bfloat16)
    first_mixed = contract(owned_rows, got_blocks, got_codes)
    owner_total = lax.psum(
        jnp.einsum("wrk,wkn->rn", first_mixed, mixing, preferred_element_type=jnp.float32).astype(
            jnp.bfloat16
        ),
        "grp",
    ).astype(jnp.float32)
    owner_first = (owner_total * owner_mask).astype(jnp.bfloat16)
    first_product = lax.dynamic_slice_in_dim(
        owner_first, lax.axis_index("grp") * share_count, share_count, 0
    )
    widened = first_product.astype(jnp.float32)
    squares = lax.psum(jnp.sum(widened * widened), ("sector", "grp"))
    inverse_norm = lax.rsqrt(squares / entry_count + epsilon)
    second_mixed = contract(owner_first, got_blocks, got_codes)
    second_product = (channel_share(second_mixed, mixing) * inverse_norm * share_mask).astype(
        jnp.bfloat16
    )
    return (first_product, second_product)


def solution(mesh):
    in_specs = (
        P(("sector", "grp"), None),
        P("sector"),
        P("grp", "sector", None, None),
        P("grp", "sector", None),
        P("grp", "sector"),
        P("grp", "sector"),
        P("grp", None),
        P("grp", None),
        P("grp", None),
        P("grp", None),
    )
    out_specs = (P(("sector", "grp"), None), P(("sector", "grp"), None))
    return jax.shard_map(local, mesh=mesh, in_specs=in_specs, out_specs=out_specs, check_vma=False)
```

profile of v0, /device:TPU:4, one launch (start us, length us, event | category | flops | bytes accessed | tf_op | source)
XLA Modules:
  0.0 513.1 jit_solution(16789400535820442056)
XLA Ops:
  7.2 0.8 fusion.28
  8.0 0.9 select_reduce_fusion.1
  8.8 0.7 fusion.38
  9.5 0.7 add_add_fusion
  10.4 0.6 copy.24
  11.0 9.1 %all-to-all-start = ((s32[2,16,2]{2,0,1:T(2,128)}), s32[2,16,2]{2,0,1:T(2,128)S(1)}, u32[]{:S(2)}, u32[]{:S(2)}) async-start(s32[2,16,2]{2,0,1:T(2,128)} %copy.24), calls=%async_computation | async-start | bytes 32768 | tf_op jit(solution)/shard_map/all_to_all | solution.py:118
  20.2 3.7 reshape.113
  23.9 2.2 convolution_convert_fusion
  26.1 2.7 reshape.114
  28.8 5.5 %copy.25 = bf16[2,16,2,16384]{3,2,0,1:T(2,128)(2,1)} copy(bf16[2,16,2,16384]{3,2,1,0:T(2,128)(2,1)} %reshape.114) | data formatting | bytes 4194304 | tf_op jit(solution)/shard_map/reshape | solution.py:112
  34.2 7.4 %all-to-all-start.1 = ((bf16[2,16,2,16384]{3,2,0,1:T(2,128)(2,1)}), bf16[2,16,2,16384]{3,2,0,1:T(2,128)(2,1)S(1)}, u32[]{:S(2)}, u32[]{:S(2)}) async-start(bf16[2,16,2,16384]{3,2,0,1:T(2,128)(2,1)} %copy.25), calls=%async_computation.1 | async-start | bytes 4194304 | tf_op jit(solution)/shard_map/all_to_all | solution.py:111
  41.7 34.9 %all-gather = bf16[32,2,1024]{2,1,0:T(2,128)(2,1)S(1)} all-gather(bf16[1,2,1024]{2,1,0:T(2,128)(2,1)S(1)} %bitcast.91), channel_id=1, replica_groups=mesh['sector'=16,'grp'=32] {'grp'}, dimensions={0}, use_global_device_ids=true | all-gather | bytes 135168 | tf_op jit(solution)/shard_map/all_gather | solution.py:71
  76.6 10.0 %reshape.119 = bf16[64,64,4,4]{3,2,1,0:T(4,128)(2,1)} reshape(bf16[32,2,1024]{2,1,0:T(2,128)(2,1)S(1)} %all-gather) | data formatting | bytes 262144 | tf_op jit(solution)/shard_map/reshape | solution.py:80
  86.6 6.4 %copy.34 = bf16[64,64,4,4,1,1]{1,0,3,2,5,4:T(8,128)(2,1)S(1)} copy(bf16[64,64,4,4,1,1]{3,2,1,0,5,4:T(4,128)(2,1)} %bitcast.79) | data formatting | bytes 262144 | tf_op jit(solution)/shard_map/reshape | solution.py:80
  94.1 27.6 %all-gather.1 = bf16[32,2,1024]{2,1,0:T(2,128)(2,1)S(1)} all-gather(bf16[1,2,1024]{2,1,0:T(2,128)(2,1)S(1)} %bitcast.92), channel_id=1, replica_groups=mesh['sector'=16,'grp'=32] {'grp'}, dimensions={0}, use_global_device_ids=true | all-gather | bytes 135168 | tf_op jit(solution)/shard_map/all_gather | solution.py:72
  122.2 4.3 reshape.121
  126.6 9.0 %copy.32 = bf16[2,16,32,16,32]{4,3,2,1,0:T(8,128)(2,1)} copy(bf16[2,16,32,16,32]{4,2,1,3,0:T(8,128)(2,1)} %bitcast.78) | data formatting | bytes 2097152 | tf_op jit(solution)/shard_map/transpose | solution.py:91
  135.5 6.8 %reshape.122 = bf16[2,512,512]{2,1,0:T(8,128)(2,1)} reshape(bf16[2,16,32,16,32]{4,3,2,1,0:T(8,128)(2,1)} %copy.32) | data formatting | bytes 2097152 | tf_op jit(solution)/shard_map/reshape | solution.py:92
  142.4 32.7 %all_gather.9 = bf16[512,512]{1,0:T(8,128)(2,1)} all-gather(bf16[16,512]{1,0:T(8,128)(2,1)S(1)} %copy-done.2), channel_id=1, replica_groups=mesh['sector'=16,'grp'=32] {'grp'}, dimensions={0}, use_global_device_ids=true | all-gather | bytes 540672 | tf_op jit(solution)/shard_map/all_gather | solution.py:38
  175.6 2.4 fusion.42
  178.0 1.5 reshape_squeeze.5
  180.4 0.4 reshape_squeeze.4
  181.9 0.5 fusion.3
  182.5 0.5 fusion.2
  183.1 1.5 fusion
  184.7 206.9 %all-reduce.2.cloned.1.call-done = bf16[512,512]{1,0:T(8,128)(2,1)} async-done(((bf16[512,512]{1,0:T(8,128)(2,1)}), bf16[512,512]{1,0:T(8,128)(2,1)}) %all-reduce.2.cloned.1.call-update) | async-done | bytes 524304 | tf_op jit(solution)/shard_map/psum | solution.py:134
  391.6 1.2 multiply_convert_fusion
  393.7 1.5 fusion.1
  395.3 1.2 multiply_reduce_fusion
  396.5 104.5 %psum.15 = f32[]{:T(128)} all-reduce(f32[]{:T(128)} %get-tuple-element.6), channel_id=1, replica_groups=mesh['sector'=16,'grp'=32] {'sector','grp'}, use_global_device_ids=true, to_apply=%region_6.7 | all-reduce | flops 1 | bytes 8 | tf_op jit(solution)/shard_map/psum | solution.py:145
  501.7 3.2 reduce-scatter.2.cloned.1.call-done
  504.9 1.4 multiply_convert_fusion.1
  (50 shorter events, 5.4 us)
Async XLA Ops:
  11.0 23.2 %all-to-all-start = ((s32[2,16,2]{2,0,1:T(2,128)}), s32[2,16,2]{2,0,1:T(2,128)S(1)}, u32[]{:S(2)}, u32[]{:S(2)}) async-start(s32[2,16,2]{2,0,1:T(2,128)} %copy.24), calls=%async_computation | async-start | bytes 32768 | tf_op jit(solution)/shard_map/all_to_all | solution.py:118
  34.2 7.5 %copy-start.3 = (bf16[2,1024]{1,0:T(2,128)(2,1)S(1)}, bf16[2,1024]{1,0:T(2,128)(2,1)}, u32[]{:S(2)}) copy-start(bf16[2,1024]{1,0:T(2,128)(2,1)} %param.18) | copy-start | bytes 12292
  34.2 141.4 %all-to-all-start.1 = ((bf16[2,16,2,16384]{3,2,0,1:T(2,128)(2,1)}), bf16[2,16,2,16384]{3,2,0,1:T(2,128)(2,1)S(1)}, u32[]{:S(2)}, u32[]{:S(2)}) async-start(bf16[2,16,2,16384]{3,2,0,1:T(2,128)(2,1)} %copy.25), calls=%async_computation.1 | async-start | bytes 4194304 | tf_op jit(solution)/shard_map/all_to_all | solution.py:111
  41.7 349.9 %all-reduce.2.cloned.1.call-start = ((), (), s32[]{:S(2)}) async-start(), calls=%async_computation.3 | async-start | bytes 1048576 | tf_op jit(solution)/shard_map/psum | solution.py:134
  86.5 6.5 %copy-start.7 = (s32[2,64]{1,0:T(2,128)S(1)}, s32[2,64]{1,0:T(2,128)}, u32[]{:S(2)}) copy-start(s32[2,64]{1,0:T(2,128)} %param.17) | copy-start | bytes 1540
  86.6 6.9 %copy-start.4 = (bf16[2,1024]{1,0:T(2,128)(2,1)S(1)}, bf16[2,1024]{1,0:T(2,128)(2,1)}, u32[]{:S(2)}) copy-start(bf16[2,1024]{1,0:T(2,128)(2,1)} %param.16) | copy-start | bytes 12292
  86.6 7.5 %copy-start.5 = (bf16[2,1024]{1,0:T(2,128)(2,1)S(1)}, bf16[2,1024]{1,0:T(2,128)(2,1)}, u32[]{:S(2)}) copy-start(bf16[2,1024]{1,0:T(2,128)(2,1)} %param.19) | copy-start | bytes 12292
  135.5 6.8 %copy-start.6 = (s32[4]{0:T(128)S(1)}, s32[4]{0:T(128)}, u32[]{:S(2)}) copy-start(s32[4]{0:T(128)} %param.11) | copy-start | bytes 52
  135.5 6.9 %copy-start.2 = (bf16[16,512]{1,0:T(8,128)(2,1)S(1)}, bf16[16,512]{1,0:T(8,128)(2,1)}, u32[]{:S(2)}) copy-start(bf16[16,512]{1,0:T(8,128)(2,1)} %param.10) | copy-start | bytes 49156
  180.9 1.0 copy-start.1
  181.8 1.2 copy-start
  184.6 320.2 %reduce-scatter.2.cloned.1.call-start = ((), (), s32[]{:S(2)}) async-start(), calls=%async_computation.4 | async-start | bytes 540672 | tf_op jit(solution)/shard_map/reduce_scatter | solution.py:42
Sparse Core Ops, SparseCore 0:
  184.8 206.7 all-reduce.1
  395.3 109.4 reduce-scatter.1
where the time goes:
time: 514 us; the launch traced here: 513 us
  waiting for transfers between devices  210 us (41%)
  blocking collectives  200 us (39%)
  local copies, waits for them, and re-layouts  55.9 us (11%)
  starting transfers between devices  16.6 us (3%)
  between operations  15 us (3%)
  matrix products  8.67 us (2%)
  other arithmetic  7.16 us (1%)
    psum x1, waiting for transfers between devices, local(): lax.psum(jnp.einsum('wrk,wkn->rn', first_mixed, mixing, preferred_element...  207 us
    psum x1, blocking collectives, local(): squares = lax.psum(jnp.sum(widened * widened), ('sector', 'grp'))  105 us
    all_gather x1, blocking collectives, local(): lax.all_gather(site_right, 'grp', axis=0, tiled=True)  34.9 us
    all_gather x1, blocking collectives, owner_gather(): return lax.all_gather(share_rows, 'grp', axis=0, tiled=True)  32.7 us
    all_gather x1, blocking collectives, local(): lax.all_gather(right_env, 'grp', axis=0, tiled=True)  27.6 us
    reshape x2, local copies, waits for them, and re-layouts, local(): right_site.reshape(WM, WM, D1, D1)  16.4 us
  transfers between devices with their start and end apart: 4, of which 2 were waited for; matrix products, arithmetic and copies ran while one was open for 11% of the time, Pallas kernels for 0%

commit v1 on v0

--- a/solution.py
+++ b/solution.py
@@ -11,6 +11,12 @@
 CAP = 2
 PHYS = 16
 epsilon = 1e-06
+
+
+def gather_and_add(shard, name):
+    pieces = lax.all_gather(shard, name, axis=0, tiled=False)
+    acc = pieces.sum(axis=0)
+    return acc
 
 
 def contract(owned_rows, got_blocks, got_codes):
@@ -131,7 +137,7 @@
     entry_count = float(sectors * groups * share_count * columns)
     owned_rows = owner_gather(start_vector) * owner_mask.astype(jnp.bfloat16)
     first_mixed = contract(owned_rows, got_blocks, got_codes)
-    owner_total = lax.psum(
+    owner_total = gather_and_add(
         jnp.einsum("wrk,wkn->rn", first_mixed, mixing, preferred_element_type=jnp.float32).astype(
             jnp.bfloat16
         ),

time: 514 us -> 416 us (0.81)
  the two profiles are of different devices: /device:TPU:4 before, /device:TPU:2 now
where the time goes in v1:
time: 416 us; the launch traced here: 415 us
  blocking collectives  197 us (47%)
  waiting for transfers between devices  107 us (26%)
  local copies, waits for them, and re-layouts  55.9 us (13%)
  starting transfers between devices  16.7 us (4%)
  other arithmetic  15 us (4%)
  between operations  15 us (4%)
  matrix products  8.66 us (2%)
    all_gather x1, waiting for transfers between devices, gather_and_add(): pieces = lax.all_gather(shard, name, axis=0, tiled=False)  103 us
    psum x1, blocking collectives, local(): squares = lax.psum(jnp.sum(widened * widened), ('sector', 'grp'))  102 us
    all_gather x1, blocking collectives, local(): lax.all_gather(site_right, 'grp', axis=0, tiled=True)  34.9 us
    all_gather x1, blocking collectives, owner_gather(): return lax.all_gather(share_rows, 'grp', axis=0, tiled=True)  32.7 us
    all_gather x1, blocking collectives, local(): lax.all_gather(right_env, 'grp', axis=0, tiled=True)  27.6 us
    reshape x2, local copies, waits for them, and re-layouts, local(): right_site.reshape(WM, WM, D1, D1)  16.4 us
    all_to_all x1, starting transfers between devices, local(): lax.all_to_all(slot_codes.reshape(channels, sectors, CAP), 'sector', spli...  9.16 us
    transpose x1, local copies, waits for them, and re-layouts, local(): mixing = mixing.reshape(channels, PHYS, PHYS, RB, RB).transpose(0, 2, 3,...  8.97 us
  transfers between devices with their start and end apart: 4, of which 2 were waited for; matrix products, arithmetic and copies ran while one was open for 13% of the time, Pallas kernels for 0%

profile of v1, /device:TPU:2, one launch (start us, length us, event | category | flops | bytes accessed | tf_op | source)
XLA Modules:
  0.0 414.7 jit_solution(12863901055881200200)
XLA Ops:
  7.2 0.8 fusion.28
  8.0 0.9 select_reduce_fusion.1
  8.8 0.7 fusion.38
  9.5 0.7 add_add_fusion
  10.4 0.6 copy.24
  11.0 9.2 %all-to-all-start = ((s32[2,16,2]{2,0,1:T(2,128)}), s32[2,16,2]{2,0,1:T(2,128)S(1)}, u32[]{:S(2)}, u32[]{:S(2)}) async-start(s32[2,16,2]{2,0,1:T(2,128)} %copy.24), calls=%async_computation | async-start | bytes 32768 | tf_op jit(solution)/shard_map/all_to_all | solution.py:124
  20.2 3.7 reshape.113
  23.9 2.2 convolution_convert_fusion
  26.1 2.7 reshape.114
  28.8 5.5 %copy.25 = bf16[2,16,2,16384]{3,2,0,1:T(2,128)(2,1)} copy(bf16[2,16,2,16384]{3,2,1,0:T(2,128)(2,1)} %reshape.114) | data formatting | bytes 4194304 | tf_op jit(solution)/shard_map/reshape | solution.py:118
  34.3 7.4 %all-to-all-start.1 = ((bf16[2,16,2,16384]{3,2,0,1:T(2,128)(2,1)}), bf16[2,16,2,16384]{3,2,0,1:T(2,128)(2,1)S(1)}, u32[]{:S(2)}, u32[]{:S(2)}) async-start(bf16[2,16,2,16384]{3,2,0,1:T(2,128)(2,1)} %copy.25), calls=%async_computation.1 | async-start | bytes 4194304 | tf_op jit(solution)/shard_map/all_to_all | solution.py:117
  41.7 34.9 %all-gather.1 = bf16[32,2,1024]{2,1,0:T(2,128)(2,1)S(1)} all-gather(bf16[1,2,1024]{2,1,0:T(2,128)(2,1)S(1)} %bitcast.93), channel_id=1, replica_groups=mesh['sector'=16,'grp'=32] {'grp'}, dimensions={0}, use_global_device_ids=true | all-gather | bytes 135168 | tf_op jit(solution)/shard_map/all_gather | solution.py:77
  76.6 10.0 %reshape.119 = bf16[64,64,4,4]{3,2,1,0:T(4,128)(2,1)} reshape(bf16[32,2,1024]{2,1,0:T(2,128)(2,1)S(1)} %all-gather.1) | data formatting | bytes 262144 | tf_op jit(solution)/shard_map/reshape | solution.py:86
  86.6 6.4 %copy.34 = bf16[64,64,4,4,1,1]{1,0,3,2,5,4:T(8,128)(2,1)S(1)} copy(bf16[64,64,4,4,1,1]{3,2,1,0,5,4:T(4,128)(2,1)} %bitcast.81) | data formatting | bytes 262144 | tf_op jit(solution)/shard_map/reshape | solution.py:86
  94.1 27.6 %all-gather.2 = bf16[32,2,1024]{2,1,0:T(2,128)(2,1)S(1)} all-gather(bf16[1,2,1024]{2,1,0:T(2,128)(2,1)S(1)} %bitcast.94), channel_id=1, replica_groups=mesh['sector'=16,'grp'=32] {'grp'}, dimensions={0}, use_global_device_ids=true | all-gather | bytes 135168 | tf_op jit(solution)/shard_map/all_gather | solution.py:78
  122.2 4.3 %reshape.121 = bf16[2,16,16,32,32]{4,3,2,1,0:T(8,128)(2,1)} reshape(bf16[2,256,1024]{2,1,0:T(8,128)(2,1)S(1)} %convolution_convert_fusion.3) | data formatting | bytes 2097152 | tf_op jit(solution)/shard_map/reshape | solution.py:96
  126.6 9.0 %copy.32 = bf16[2,16,32,16,32]{4,3,2,1,0:T(8,128)(2,1)} copy(bf16[2,16,32,16,32]{4,2,1,3,0:T(8,128)(2,1)} %bitcast.80) | data formatting | bytes 2097152 | tf_op jit(solution)/shard_map/transpose | solution.py:97
  135.6 6.8 %reshape.122 = bf16[2,512,512]{2,1,0:T(8,128)(2,1)} reshape(bf16[2,16,32,16,32]{4,3,2,1,0:T(8,128)(2,1)} %copy.32) | data formatting | bytes 2097152 | tf_op jit(solution)/shard_map/reshape | solution.py:98
  142.5 32.7 %all_gather.15 = bf16[512,512]{1,0:T(8,128)(2,1)} all-gather(bf16[16,512]{1,0:T(8,128)(2,1)S(1)} %copy-done.4), channel_id=1, replica_groups=mesh['sector'=16,'grp'=32] {'grp'}, dimensions={0}, use_global_device_ids=true | all-gather | bytes 540672 | tf_op jit(solution)/shard_map/all_gather | solution.py:44
  175.7 2.4 fusion.42
  178.1 1.5 reshape_squeeze.4
  180.5 0.4 reshape_squeeze.5
  182.0 0.5 fusion.2
  182.5 0.5 fusion.3
  183.1 1.5 fusion
  184.7 102.6 %all-gather.5.cloned.1.call-done = bf16[16384,512]{1,0:T(8,128)(2,1)} async-done(((bf16[512,512]{1,0:T(8,128)(2,1)}), bf16[16384,512]{1,0:T(8,128)(2,1)}) %all-gather.5.cloned.1.call-update) | async-done | bytes 16777232 | tf_op jit(solution)/shard_map/all_gather | solution.py:17
  287.3 8.8 %reduce_sum.44 = bf16[512,512]{1,0:T(8,128)(2,1)S(1)} reduce(bf16[32,512,512]{2,1,0:T(8,128)(2,1)} %bitcast.79, bf16[]{:T(256)} %constant.11.clone.1), dimensions={0}, to_apply=%region_3.4 | reduce | flops 8126464 | bytes 17301506 | tf_op jit(solution)/shard_map/reduce_sum | solution.py:18
  297.2 1.5 fusion.1
  298.8 1.2 multiply_reduce_fusion
  300.0 101.8 %psum.7 = f32[]{:T(128)} all-reduce(f32[]{:T(128)} %get-tuple-element.6), channel_id=1, replica_groups=mesh['sector'=16,'grp'=32] {'sector','grp'}, use_global_device_ids=true, to_apply=%region_6.7 | all-reduce | flops 1 | bytes 8 | tf_op jit(solution)/shard_map/psum | solution.py:151
  402.5 4.0 reduce-scatter.2.cloned.1.call-done
  406.5 1.4 multiply_convert_fusion.1
  (55 shorter events, 5.6 us)
Async XLA Ops:
  11.0 23.2 %all-to-all-start = ((s32[2,16,2]{2,0,1:T(2,128)}), s32[2,16,2]{2,0,1:T(2,128)S(1)}, u32[]{:S(2)}, u32[]{:S(2)}) async-start(s32[2,16,2]{2,0,1:T(2,128)} %copy.24), calls=%async_computation | async-start | bytes 32768 | tf_op jit(solution)/shard_map/all_to_all | solution.py:124
  34.3 7.5 %copy-start.5 = (bf16[2,1024]{1,0:T(2,128)(2,1)S(1)}, bf16[2,1024]{1,0:T(2,128)(2,1)}, u32[]{:S(2)}) copy-start(bf16[2,1024]{1,0:T(2,128)(2,1)} %param.18) | copy-start | bytes 12292
  34.3 141.4 %all-to-all-start.1 = ((bf16[2,16,2,16384]{3,2,0,1:T(2,128)(2,1)}), bf16[2,16,2,16384]{3,2,0,1:T(2,128)(2,1)S(1)}, u32[]{:S(2)}, u32[]{:S(2)}) async-start(bf16[2,16,2,16384]{3,2,0,1:T(2,128)(2,1)} %copy.25), calls=%async_computation.1 | async-start | bytes 4194304 | tf_op jit(solution)/shard_map/all_to_all | solution.py:117
  41.7 245.6 %all-gather.5.cloned.1.call-start = ((), (), s32[]{:S(2)}) async-start(), calls=%async_computation.4 | async-start | bytes 17301504 | tf_op jit(solution)/shard_map/all_gather | solution.py:17
  86.6 6.5 %copy-start.9 = (s32[2,64]{1,0:T(2,128)S(1)}, s32[2,64]{1,0:T(2,128)}, u32[]{:S(2)}) copy-start(s32[2,64]{1,0:T(2,128)} %param.17) | copy-start | bytes 1540
  86.6 6.9 %copy-start.6 = (bf16[2,1024]{1,0:T(2,128)(2,1)S(1)}, bf16[2,1024]{1,0:T(2,128)(2,1)}, u32[]{:S(2)}) copy-start(bf16[2,1024]{1,0:T(2,128)(2,1)} %param.16) | copy-start | bytes 12292
  86.6 7.5 %copy-start.7 = (bf16[2,1024]{1,0:T(2,128)(2,1)S(1)}, bf16[2,1024]{1,0:T(2,128)(2,1)}, u32[]{:S(2)}) copy-start(bf16[2,1024]{1,0:T(2,128)(2,1)} %param.19) | copy-start | bytes 12292
  135.6 6.8 %copy-start.8 = (s32[4]{0:T(128)S(1)}, s32[4]{0:T(128)}, u32[]{:S(2)}) copy-start(s32[4]{0:T(128)} %param.11) | copy-start | bytes 52
  135.6 6.9 %copy-start.4 = (bf16[16,512]{1,0:T(8,128)(2,1)S(1)}, bf16[16,512]{1,0:T(8,128)(2,1)}, u32[]{:S(2)}) copy-start(bf16[16,512]{1,0:T(8,128)(2,1)} %param.10) | copy-start | bytes 49156
  180.5 1.4 copy-start.2
  180.9 1.0 copy-start.1
  181.9 1.2 copy-start
  184.7 221.8 %reduce-scatter.2.cloned.1.call-start = ((), (), s32[]{:S(2)}) async-start(), calls=%async_computation.3 | async-start | bytes 540672 | tf_op jit(solution)/shard_map/reduce_scatter | solution.py:48
  287.3 9.0 %copy-start.3 = (bf16[4,4,128,128]{3,1,2,0:T(4,128)(2,1)S(1)}, bf16[4,4,128,128]{3,1,2,0:T(4,128)(2,1)}, u32[]{:S(2)}) copy-start(bf16[4,4,128,128]{3,1,2,0:T(4,128)(2,1)} %copy-done.2) | copy-start | bytes 1572868
Sparse Core Ops, SparseCore 0:
  184.8 102.4 all-gather.4
  298.8 107.6 reduce-scatter.1
